TPU v7x, 32 devices: a whole 2x2x4 slice. The times are simulated.
32 devices in a mesh: gx: 4 (over z), gy: 8 (over y, x, core).
Axes of the slice: x: 2, y: 2, z: 4, core: 2. Of those that a mesh axis runs over, the one named last changes fastest.
Arguments:
- conductivity: bfloat16 [2, 1024, 4096], P(None, 'gy', 'gx'), may hold values from 0.099609375 to 1.59375
Outputs:
- coarse_stencil: float32 [9, 8, 64, 2048], P(None, 'gy', 'gx')
All inputs are finite; a program needn't handle non-finite values.
Results may differ from a plain program's by a relative error of at most 0.0003.
Values may be sent and summed in bfloat16 or wider, within the bound.
A program may use at most 64 MiB of HBM per device.

v0:
```python
from functools import partial
import jax
import jax.numpy as jnp
from jax import lax
from jax.sharding import PartitionSpec as P


def with_halo(cells, sides, width):
    for axis, dim in sides:
        count = lax.axis_size(axis)
        ends = count - 1
        head = lax.slice_in_dim(cells, 0, width, axis=dim)
        tail = lax.slice_in_dim(cells, cells.shape[dim] - width, cells.shape[dim], axis=dim)
        cells = jnp.concatenate(
            [
                lax.ppermute(tail, axis, [(i, (i + 1) % count) for i in range(ends)]),
                cells,
                lax.ppermute(head, axis, [((i + 1) % count, i) for i in range(ends)]),
            ],
            axis=dim,
        )
    return cells


def harmonic(first, second):
    return 2.0 * first * second / (first + second)


def prepare_window(extended, row_start, col_start, rows_all, cols_all, used_rows, used_cols):
    conduct = extended.astype(jnp.float32)
    ext_rows = conduct.shape[1]
    ext_cols = conduct.shape[2]
    row_places = jnp.arange(ext_rows, dtype=jnp.int32)
    col_places = jnp.arange(ext_cols, dtype=jnp.int32)
    row_ids = row_start - 2 + row_places
    col_ids = col_start - 2 + col_places
    row_inside = (row_ids >= 0) & (row_ids < rows_all) & (row_places < used_rows)
    col_inside = (col_ids >= 0) & (col_ids < cols_all) & (col_places < used_cols)
    inside = row_inside[:, None] & col_inside[None, :]
    safe_values = jnp.where(inside[None], conduct, 1.0)
    east_face = jnp.where(
        jnp.roll(inside, -1, 1)[None],
        harmonic(safe_values, jnp.roll(safe_values, -1, 2)),
        safe_values,
    )
    west_face = jnp.where(
        jnp.roll(inside, 1, 1)[None],
        harmonic(safe_values, jnp.roll(safe_values, 1, 2)),
        safe_values,
    )
    north_face = jnp.where(
        jnp.roll(inside, -1, 0)[None],
        harmonic(safe_values, jnp.roll(safe_values, -1, 1)),
        safe_values,
    )
    south_face = jnp.where(
        jnp.roll(inside, 1, 0)[None],
        harmonic(safe_values, jnp.roll(safe_values, 1, 1)),
        safe_values,
    )
    vertical = harmonic(safe_values[0], safe_values[1])
    centre = east_face + west_face + north_face + south_face + vertical[None] + safe_values
    col_east = east_face[0] + east_face[1]
    col_west = west_face[0] + west_face[1]
    row_north = north_face[0] + north_face[1]
    row_south = south_face[0] + south_face[1]
    left_weight = col_west / (col_west + col_east)
    right_weight = col_east / (col_west + col_east)
    south_weight = row_south / (row_south + row_north)
    north_weight = row_north / (row_south + row_north)
    odd_rows = (row_ids % 2 == 1)[:, None]
    odd_cols = (col_ids % 2 == 1)[None, :]
    even_point = inside & (row_ids % 2 == 0)[:, None] & (col_ids % 2 == 0)[None, :]
    row_class = (row_ids // 2 % 3)[:, None]
    col_class = (col_ids // 2 % 3)[None, :]
    return (
        inside,
        odd_rows,
        odd_cols,
        even_point,
        row_class,
        col_class,
        east_face,
        west_face,
        north_face,
        south_face,
        vertical,
        centre,
        left_weight,
        right_weight,
        south_weight,
        north_weight,
    )


def probe_rows(prepared, local_rows, colour):
    (
        inside,
        odd_rows,
        odd_cols,
        even_point,
        row_class,
        col_class,
        east_face,
        west_face,
        north_face,
        south_face,
        vertical,
        centre,
        left_weight,
        right_weight,
        south_weight,
        north_weight,
    ) = prepared
    chosen = even_point & (row_class == colour // 3) & (col_class == colour % 3)
    probe_field = chosen.astype(jnp.float32)
    along_x = jnp.where(
        odd_cols,
        left_weight * jnp.roll(probe_field, 1, 1) + right_weight * jnp.roll(probe_field, -1, 1),
        probe_field,
    )
    fine_field = jnp.where(
        odd_rows,
        south_weight * jnp.roll(along_x, 1, 0) + north_weight * jnp.roll(along_x, -1, 0),
        along_x,
    )
    fine_field = jnp.where(inside, fine_field, 0.0)
    applied = (
        centre * fine_field
        - east_face * jnp.roll(fine_field, -1, 1)
        - west_face * jnp.roll(fine_field, 1, 1)
        - north_face * jnp.roll(fine_field, -1, 0)
        - south_face * jnp.roll(fine_field, 1, 0)
        - vertical * fine_field
    )
    folded = jnp.where(inside, applied[0] + applied[1], 0.0)
    rows_done = (
        folded + jnp.roll(south_weight * folded, -1, 0) + jnp.roll(north_weight * folded, 1, 0)
    )
    cols_done = (
        rows_done
        + jnp.roll(left_weight * rows_done, -1, 1)
        + jnp.roll(right_weight * rows_done, 1, 1)
    )
    width = cols_done.shape[1]
    kept = cols_done[2 : 2 + local_rows].reshape(local_rows // 2, 2, width)
    return kept[:, 0]


def by_offset(colours, row_first, col_first):
    count_rows = colours.shape[1]
    count_cols = colours.shape[2]
    coarse_rows = row_first + jnp.arange(count_rows, dtype=jnp.int32)
    coarse_cols = col_first + jnp.arange(count_cols, dtype=jnp.int32)
    fields = []
    for step_row in (-1, 0, 1):
        for step_col in (-1, 0, 1):
            row_group = (coarse_rows + step_row) % 3
            col_group = (coarse_cols + step_col) % 3
            selected = jnp.zeros((count_rows, count_cols), jnp.float32)
            for colour in range(9):
                chosen = (row_group == colour // 3)[:, None] & (col_group == colour % 3)[None, :]
                selected = jnp.where(chosen, colours[colour], selected)
            fields.append(selected)
    return jnp.stack(fields)


def shards(conductivity):
    local_rows = conductivity.shape[1]
    local_cols = conductivity.shape[2]
    row_start = lax.axis_index("gy") * local_rows
    col_start = lax.axis_index("gx") * local_cols
    rows_all = local_rows * lax.axis_size("gy")
    cols_all = local_cols * lax.axis_size("gx")
    extended = with_halo(conductivity, (("gx", 2), ("gy", 1)), 2)
    used_rows = local_rows + 4
    used_cols = local_cols + 4
    row_fill = -used_rows % 8
    col_fill = -used_cols % 128
    aligned = jnp.pad(extended, ((0, 0), (0, row_fill), (0, col_fill)))
    prepared = prepare_window(
        aligned, row_start, col_start, rows_all, cols_all, used_rows, used_cols
    )
    row_picked = lax.map(partial(probe_rows, prepared, local_rows), jnp.arange(9, dtype=jnp.int32))
    width = row_picked.shape[2]
    half_cols = local_cols // 2
    picker = (
        jnp.arange(width, dtype=jnp.int32)[:, None]
        == 2 + 2 * jnp.arange(half_cols, dtype=jnp.int32)[None, :]
    ).astype(jnp.float32)
    flat_rows = row_picked.reshape(9 * (local_rows // 2), width)
    colours = jnp.dot(
        flat_rows, picker, precision=lax.Precision.HIGHEST, preferred_element_type=jnp.float32
    )
    colours = colours.reshape(9, local_rows // 2, half_cols)
    stencil = by_offset(colours, row_start // 2, col_start // 2)
    moved = lax.all_to_all(stencil, "gx", split_axis=1, concat_axis=2, tiled=True)
    return moved[:, None]


def solution(mesh):
    in_specs = (P(None, "gy", "gx"),)
    out_specs = P(None, "gy", "gx", None)
    return jax.shard_map(shards, mesh=mesh, in_specs=in_specs, out_specs=out_specs, check_vma=False)
```

profile of v0, /device:TPU:4, one launch (start us, length us, event | category | flops | bytes accessed | tf_op | source)
XLA Modules:
  0.0 210.9 jit_solution(8876209915577884419)
XLA Ops:
  0.0 1.0 fusion.78
  1.0 3.5 %collective-permute-start = (bf16[2,128,2]{2,1,0:T(8,128)(2,1)S(1)}, bf16[2,128,2]{2,1,0:T(8,128)(2,1)S(1)}, u32[]{:S(2)}, u32[]{:S(2)}) collective-permute-start(bf16[2,128,2]{2,1,0:T(8,128)(2,1)S(1)} %get-tuple-element.442), channel_id=1, source_target_pairs={{0,8},{8,16},{16,24},{1,9},{9,17},{17,25},{2,10},{10,18},{18,26},{... | collective-permute-start | bytes 3080 | tf_op jit(solution)/shard_map/ppermute | solution.py:16
  4.5 1.3 collective-permute-start.1
  7.1 3.5 %collective-permute-done.1 = bf16[2,128,2]{2,1,0:T(8,128)(2,1)S(1)} collective-permute-done((bf16[2,128,2]{2,1,0:T(8,128)(2,1)S(1)}, bf16[2,128,2]{2,1,0:T(8,128)(2,1)S(1)}, u32[]{:S(2)}, u32[]{:S(2)}) %collective-permute-start.1) | collective-permute-done | bytes 1056 | tf_op jit(solution)/shard_map/ppermute | solution.py:18
  11.3 1.9 collective-permute-start.2
  13.2 4.5 %collective-permute-start.3 = (bf16[2,2,1028]{2,1,0:T(2,128)(2,1)S(1)}, bf16[2,2,1028]{2,1,0:T(2,128)(2,1)S(1)}, u32[]{:S(2)}, u32[]{:S(2)}) collective-permute-start(bf16[2,2,1028]{2,1,0:T(2,128)(2,1)S(1)} %get-tuple-element.440), channel_id=1, source_target_pairs={{1,0},{2,1},{3,2},{4,3},{5,4},{6,5},{7,6},{9,8},{10,9},{11,10},{12... | collective-permute-start | bytes 24680 | tf_op jit(solution)/shard_map/ppermute | solution.py:18
  17.8 1.3 collective-permute-done.3
  20.2 0.9 fusion.39
  21.1 4.2 %add_add_fusion = (f32[2,136,1152]{2,1,0:T(8,128)}, f32[2,136,1152]{2,1,0:T(8,128)S(1)}, f32[2,136,1152]{2,1,0:T(8,128)S(1)}, f32[2,136,1152]{2,1,0:T(8,128)S(1)}, f32[2,136,1152]{2,1,0:T(8,128)S(1)}) fusion(f32[136,1152]{1,0:T(8,128)S(1)} %divide_bitcast_fusion, pred[136,1152]{1,0:T(8,128)(4,1)S(1)} %broadcast_and_fusion, ...), kind=kLoop, calls=%fused_computation.66 | loop fusion | flops 13160448 | bytes 13233216 | tf_op jit(solution)/shard_map/add | solution.py:62
  25.5 0.9 copy-done
  27.6 121.1 %while.14 = (s32[]{:T(128)}, f32[9,64,1152]{2,1,0:T(8,128)}, s32[9]{0:T(128)S(1)}, f32[136,1152]{1,0:T(8,128)S(1)}, f32[136,1152]{1,0:T(8,128)S(1)}, /*index=5*/...) while((s32[]{:T(128)}, f32[9,64,1152]{2,1,0:T(8,128)}, ...), condition=%wide.region_1.2_spmd.clone.clone, body=%wide.region_0.1_spmd.clone.clone.sunk | while | flops 10339566 | bytes 78140304 | solution.py:184
  31.2 1.4 fusion.104
  33.5 0.8 copy-done.8
  35.9 0.8 subtract_subtract_fusion.2
  37.9 1.2 reshape.701
  39.1 1.3 slice_bitcast_fusion.2
  44.6 1.4 fusion.104
  47.0 0.8 copy-done.8
  49.4 0.8 subtract_subtract_fusion.2
  51.3 1.2 reshape.701
  52.5 1.3 slice_bitcast_fusion.2
  58.1 1.4 fusion.104
  60.4 0.8 copy-done.8
  62.8 0.8 subtract_subtract_fusion.2
  64.8 1.2 reshape.701
  66.0 1.3 slice_bitcast_fusion.2
  67.2 0.7 copy_dynamic-update-slice_fusion.2
  71.5 1.4 fusion.104
  73.9 0.8 copy-done.8
  76.3 0.8 subtract_subtract_fusion.2
  78.2 1.2 reshape.701
  79.4 1.3 slice_bitcast_fusion.2
  85.0 1.4 fusion.104
  87.3 0.8 copy-done.8
  89.7 0.8 subtract_subtract_fusion.2
  91.7 1.2 reshape.701
  92.9 1.3 slice_bitcast_fusion.2
  98.4 1.4 fusion.104
  100.8 0.8 copy-done.8
  103.2 0.8 subtract_subtract_fusion.2
  105.1 1.2 reshape.701
  106.3 1.3 slice_bitcast_fusion.2
  107.6 0.8 copy_dynamic-update-slice_fusion.2
  111.9 1.4 fusion.104
  114.3 0.8 copy-done.8
  116.7 0.8 subtract_subtract_fusion.2
  118.6 1.2 reshape.701
  119.8 1.3 slice_bitcast_fusion.2
  121.1 0.7 copy_dynamic-update-slice_fusion.2
  125.4 1.4 fusion.104
  127.7 0.8 copy-done.8
  130.1 0.8 subtract_subtract_fusion.2
  132.1 1.2 reshape.701
  133.2 1.3 slice_bitcast_fusion.2
  138.8 1.4 fusion.104
  141.2 0.8 copy-done.8
  143.6 0.8 subtract_subtract_fusion.2
  145.5 1.2 reshape.701
  146.7 1.3 slice_bitcast_fusion.2
  148.0 0.8 copy_dynamic-update-slice_fusion.2
  148.7 4.3 %fusion.23 = f32[576,512]{1,0:T(8,128)S(1)} fusion(f32[576,1152]{1,0:T(8,128)} %bitcast.88, s32[512]{0:T(512)S(1)} %multiply_add_fusion), kind=kOutput, calls=%fused_computation.55 | convolution fusion | flops 4077453312 | bytes 3835904 | tf_op jit(solution)/shard_map/dot_general | solution.py:192
  155.7 52.7 %all_to_all.15 = f32[9,64,512]{2,0,1:T(8,128)S(1)} all-to-all(f32[9,64,512]{2,0,1:T(8,128)S(1)} %copy.7), channel_id=1, replica_groups=mesh['gx'=4,'gy'=8] {'gx'}, dimensions={1} | all-to-all | bytes 2359296 | tf_op jit(solution)/shard_map/all_to_all | solution.py:197
  208.3 0.8 copy.8
  209.1 1.8 broadcast_in_dim.97
  (393 shorter events, 59.2 us)
Async XLA Ops:
  1.0 6.1 %collective-permute-start = (bf16[2,128,2]{2,1,0:T(8,128)(2,1)S(1)}, bf16[2,128,2]{2,1,0:T(8,128)(2,1)S(1)}, u32[]{:S(2)}, u32[]{:S(2)}) collective-permute-start(bf16[2,128,2]{2,1,0:T(8,128)(2,1)S(1)} %get-tuple-element.442), channel_id=1, source_target_pairs={{0,8},{8,16},{16,24},{1,9},{9,17},{17,25},{2,10},{10,18},{18,26},{... | collective-permute-start | bytes 3080 | tf_op jit(solution)/shard_map/ppermute | solution.py:16
  4.5 6.2 %collective-permute-start.1 = (bf16[2,128,2]{2,1,0:T(8,128)(2,1)S(1)}, bf16[2,128,2]{2,1,0:T(8,128)(2,1)S(1)}, u32[]{:S(2)}, u32[]{:S(2)}) collective-permute-start(bf16[2,128,2]{2,1,0:T(8,128)(2,1)S(1)} %get-tuple-element.441), channel_id=1, source_target_pairs={{8,0},{16,8},{24,16},{9,1},{17,9},{25,17},{10,2},{18,10},{26,18},{... | collective-permute-start | bytes 3080 | tf_op jit(solution)/shard_map/ppermute | solution.py:18
  5.9 4.7 %copy-start.9 = (bf16[2,128,1024]{2,1,0:T(8,128)(2,1)S(1)}, bf16[2,128,1024]{2,1,0:T(8,128)(2,1)}, u32[]{:S(2)}) copy-start(bf16[2,128,1024]{2,1,0:T(8,128)(2,1)} %param.3) | copy-start | bytes 1572868
  11.3 6.5 %collective-permute-start.2 = (bf16[2,2,1028]{2,1,0:T(2,128)(2,1)S(1)}, bf16[2,2,1028]{2,1,0:T(2,128)(2,1)S(1)}, u32[]{:S(2)}, u32[]{:S(2)}) collective-permute-start(bf16[2,2,1028]{2,1,0:T(2,128)(2,1)S(1)} %get-tuple-element.439), channel_id=1, source_target_pairs={{0,1},{1,2},{2,3},{3,4},{4,5},{5,6},{6,7},{8,9},{9,10},{10,11},{11... | collective-permute-start | bytes 24680 | tf_op jit(solution)/shard_map/ppermute | solution.py:16
  13.2 5.9 %collective-permute-start.3 = (bf16[2,2,1028]{2,1,0:T(2,128)(2,1)S(1)}, bf16[2,2,1028]{2,1,0:T(2,128)(2,1)S(1)}, u32[]{:S(2)}, u32[]{:S(2)}) collective-permute-start(bf16[2,2,1028]{2,1,0:T(2,128)(2,1)S(1)} %get-tuple-element.440), channel_id=1, source_target_pairs={{1,0},{2,1},{3,2},{4,3},{5,4},{6,5},{7,6},{9,8},{10,9},{11,10},{12... | collective-permute-start | bytes 24680 | tf_op jit(solution)/shard_map/ppermute | solution.py:18
  25.3 1.1 copy-start
  25.3 1.5 copy-start.2
  25.3 2.0 copy-start.4
  25.3 2.3 %copy-start.6 = (f32[2,136,1152]{2,1,0:T(8,128)}, f32[2,136,1152]{2,1,0:T(8,128)S(1)}, u32[]{:S(2)}) copy-start(f32[2,136,1152]{2,1,0:T(8,128)S(1)} %get-tuple-element.647) | copy-start | bytes 3760132
  33.0 1.3 copy-start.8
  33.3 1.5 copy-start.5
  33.3 1.9 copy-start.7
  33.4 2.2 %copy-start.1 = (f32[2,136,1152]{2,1,0:T(8,128)S(1)}, f32[2,136,1152]{2,1,0:T(8,128)}, u32[]{:S(2)}) copy-start(f32[2,136,1152]{2,1,0:T(8,128)} %get-tuple-element.698) | copy-start | bytes 3760132 | tf_op jit(solution)/shard_map/while
  33.4 2.5 %copy-start.3 = (f32[2,136,1152]{2,1,0:T(8,128)S(1)}, f32[2,136,1152]{2,1,0:T(8,128)}, u32[]{:S(2)}) copy-start(f32[2,136,1152]{2,1,0:T(8,128)} %get-tuple-element.699) | copy-start | bytes 3760132 | tf_op jit(solution)/shard_map/while
  46.5 1.3 copy-start.8
  46.7 1.5 copy-start.5
  46.7 1.9 copy-start.7
  46.8 2.2 %copy-start.1 = (f32[2,136,1152]{2,1,0:T(8,128)S(1)}, f32[2,136,1152]{2,1,0:T(8,128)}, u32[]{:S(2)}) copy-start(f32[2,136,1152]{2,1,0:T(8,128)} %get-tuple-element.698) | copy-start | bytes 3760132 | tf_op jit(solution)/shard_map/while
  46.9 2.5 %copy-start.3 = (f32[2,136,1152]{2,1,0:T(8,128)S(1)}, f32[2,136,1152]{2,1,0:T(8,128)}, u32[]{:S(2)}) copy-start(f32[2,136,1152]{2,1,0:T(8,128)} %get-tuple-element.699) | copy-start | bytes 3760132 | tf_op jit(solution)/shard_map/while
  59.9 1.3 copy-start.8
  60.2 1.5 copy-start.5
  60.2 1.9 copy-start.7
  60.3 2.2 %copy-start.1 = (f32[2,136,1152]{2,1,0:T(8,128)S(1)}, f32[2,136,1152]{2,1,0:T(8,128)}, u32[]{:S(2)}) copy-start(f32[2,136,1152]{2,1,0:T(8,128)} %get-tuple-element.698) | copy-start | bytes 3760132 | tf_op jit(solution)/shard_map/while
  60.3 2.5 %copy-start.3 = (f32[2,136,1152]{2,1,0:T(8,128)S(1)}, f32[2,136,1152]{2,1,0:T(8,128)}, u32[]{:S(2)}) copy-start(f32[2,136,1152]{2,1,0:T(8,128)} %get-tuple-element.699) | copy-start | bytes 3760132 | tf_op jit(solution)/shard_map/while
  73.4 1.3 copy-start.8
  73.6 1.5 copy-start.5
  73.6 1.9 copy-start.7
  73.7 2.2 %copy-start.1 = (f32[2,136,1152]{2,1,0:T(8,128)S(1)}, f32[2,136,1152]{2,1,0:T(8,128)}, u32[]{:S(2)}) copy-start(f32[2,136,1152]{2,1,0:T(8,128)} %get-tuple-element.698) | copy-start | bytes 3760132 | tf_op jit(solution)/shard_map/while
  73.8 2.5 %copy-start.3 = (f32[2,136,1152]{2,1,0:T(8,128)S(1)}, f32[2,136,1152]{2,1,0:T(8,128)}, u32[]{:S(2)}) copy-start(f32[2,136,1152]{2,1,0:T(8,128)} %get-tuple-element.699) | copy-start | bytes 3760132 | tf_op jit(solution)/shard_map/while
  86.8 1.3 copy-start.8
  87.1 1.5 copy-start.5
  87.1 1.9 copy-start.7
  87.2 2.2 %copy-start.1 = (f32[2,136,1152]{2,1,0:T(8,128)S(1)}, f32[2,136,1152]{2,1,0:T(8,128)}, u32[]{:S(2)}) copy-start(f32[2,136,1152]{2,1,0:T(8,128)} %get-tuple-element.698) | copy-start | bytes 3760132 | tf_op jit(solution)/shard_map/while
  87.2 2.5 %copy-start.3 = (f32[2,136,1152]{2,1,0:T(8,128)S(1)}, f32[2,136,1152]{2,1,0:T(8,128)}, u32[]{:S(2)}) copy-start(f32[2,136,1152]{2,1,0:T(8,128)} %get-tuple-element.699) | copy-start | bytes 3760132 | tf_op jit(solution)/shard_map/while
  100.3 1.3 copy-start.8
  100.5 1.5 copy-start.5
  100.5 1.9 copy-start.7
  100.6 2.2 %copy-start.1 = (f32[2,136,1152]{2,1,0:T(8,128)S(1)}, f32[2,136,1152]{2,1,0:T(8,128)}, u32[]{:S(2)}) copy-start(f32[2,136,1152]{2,1,0:T(8,128)} %get-tuple-element.698) | copy-start | bytes 3760132 | tf_op jit(solution)/shard_map/while
  100.7 2.5 %copy-start.3 = (f32[2,136,1152]{2,1,0:T(8,128)S(1)}, f32[2,136,1152]{2,1,0:T(8,128)}, u32[]{:S(2)}) copy-start(f32[2,136,1152]{2,1,0:T(8,128)} %get-tuple-element.699) | copy-start | bytes 3760132 | tf_op jit(solution)/shard_map/while
  113.8 1.3 copy-start.8
  114.0 1.5 copy-start.5
  114.0 1.9 copy-start.7
  114.1 2.2 %copy-start.1 = (f32[2,136,1152]{2,1,0:T(8,128)S(1)}, f32[2,136,1152]{2,1,0:T(8,128)}, u32[]{:S(2)}) copy-start(f32[2,136,1152]{2,1,0:T(8,128)} %get-tuple-element.698) | copy-start | bytes 3760132 | tf_op jit(solution)/shard_map/while
  114.1 2.5 %copy-start.3 = (f32[2,136,1152]{2,1,0:T(8,128)S(1)}, f32[2,136,1152]{2,1,0:T(8,128)}, u32[]{:S(2)}) copy-start(f32[2,136,1152]{2,1,0:T(8,128)} %get-tuple-element.699) | copy-start | bytes 3760132 | tf_op jit(solution)/shard_map/while
  127.2 1.3 copy-start.8
  127.5 1.5 copy-start.5
  127.5 1.9 copy-start.7
  127.6 2.2 %copy-start.1 = (f32[2,136,1152]{2,1,0:T(8,128)S(1)}, f32[2,136,1152]{2,1,0:T(8,128)}, u32[]{:S(2)}) copy-start(f32[2,136,1152]{2,1,0:T(8,128)} %get-tuple-element.698) | copy-start | bytes 3760132 | tf_op jit(solution)/shard_map/while
  127.6 2.5 %copy-start.3 = (f32[2,136,1152]{2,1,0:T(8,128)S(1)}, f32[2,136,1152]{2,1,0:T(8,128)}, u32[]{:S(2)}) copy-start(f32[2,136,1152]{2,1,0:T(8,128)} %get-tuple-element.699) | copy-start | bytes 3760132 | tf_op jit(solution)/shard_map/while
  140.7 1.3 copy-start.8
  140.9 1.5 copy-start.5
  140.9 1.9 copy-start.7
  141.0 2.2 %copy-start.1 = (f32[2,136,1152]{2,1,0:T(8,128)S(1)}, f32[2,136,1152]{2,1,0:T(8,128)}, u32[]{:S(2)}) copy-start(f32[2,136,1152]{2,1,0:T(8,128)} %get-tuple-element.698) | copy-start | bytes 3760132 | tf_op jit(solution)/shard_map/while
  141.0 2.5 %copy-start.3 = (f32[2,136,1152]{2,1,0:T(8,128)S(1)}, f32[2,136,1152]{2,1,0:T(8,128)}, u32[]{:S(2)}) copy-start(f32[2,136,1152]{2,1,0:T(8,128)} %get-tuple-element.699) | copy-start | bytes 3760132 | tf_op jit(solution)/shard_map/while
where the time goes:
time: 212 us; the launch traced here: 211 us
  local copies, waits for them, and re-layouts  74.1 us (35%)
  blocking collectives  52.7 us (25%)
  other arithmetic  46.5 us (22%)
  loops' own time  16.9 us (8%)
  starting transfers between devices  11.2 us (5%)
  waiting for transfers between devices  4.81 us (2%)
  matrix products  4.33 us (2%)
    all_to_all x1, blocking collectives, shards(): lax.all_to_all(stencil, 'gx', split_axis=1, concat_axis=2, tiled=True)  52.7 us
    while x90, local copies, waits for them, and re-layouts  21.7 us
    another operation x1, loops' own time, shards(): lax.map(partial(probe_rows, prepared, local_rows), jnp.arange(9, dtype=jn...  16.9 us
    mul x9, other arithmetic, probe_rows(): vertical * fine_field  12.9 us
    broadcast_in_dim x9, local copies, waits for them, and re-layouts, shards(): lax.map(partial(probe_rows, prepared, local_rows), jnp.arange(9, dtype=jn...  11.4 us
    reshape x9, local copies, waits for them, and re-layouts, probe_rows(): kept = cols_done[2:2 + local_rows].reshape(local_rows // 2, 2, width)  10.5 us
    sub x9, other arithmetic, probe_rows(): centre * fine_field - east_face * jnp.roll(fine_field, -1, 1)  6.98 us
    dynamic_update_slice x9, local copies, waits for them, and re-layouts, shards(): lax.map(partial(probe_rows, prepared, local_rows), jnp.arange(9, dtype=jn...  6.72 us
  transfers between devices with their start and end apart: 4, of which 2 were waited for; matrix products, arithmetic and copies ran while one was open for 1% of the time, Pallas kernels for 0%

commit v1 on v0

--- a/solution.py
+++ b/solution.py
@@ -3,6 +3,28 @@
 import jax.numpy as jnp
 from jax import lax
 from jax.sharding import PartitionSpec as P
+from jax.lax import axis_index, axis_size, ppermute
+
+
+def connect_samples(block_in, pos_dim, view):
+    view_out = block_in.shape
+    return jnp.moveaxis(
+        block_in.reshape(
+            *view_out[:pos_dim], view, view_out[pos_dim] // view, *view_out[pos_dim + 1 :]
+        ),
+        pos_dim,
+        0,
+    )
+
+
+def _attach_chains(arr, ndim_at):
+    arr = jnp.moveaxis(arr, 0, ndim_at)
+    block_next = arr.shape
+    return arr.reshape(
+        *block_next[:ndim_at],
+        block_next[ndim_at] * block_next[ndim_at + 1],
+        *block_next[ndim_at + 2 :]
+    )
 
 
 def with_halo(cells, sides, width):
@@ -166,6 +188,17 @@
 
 
 def shards(conductivity):
+
+    def settle_the_joints(values, ax_name, mine, frame_in):
+        y, state_next = (axis_size(ax_name), axis_index(ax_name))
+        current_block = connect_samples(values, mine, y)
+        stack_in = [current_block[state_next]]
+        for d in range(1, y):
+            local_now = current_block[(state_next + d) % y]
+            stack_in.append(ppermute(local_now, ax_name, [(s, (s + d) % y) for s in range(y)]))
+        current_block = jnp.stack(stack_in, axis=0)[(state_next - jnp.arange(y)) % y]
+        return _attach_chains(current_block, frame_in)
+
     local_rows = conductivity.shape[1]
     local_cols = conductivity.shape[2]
     row_start = lax.axis_index("gy") * local_rows
@@ -194,7 +227,7 @@
     )
     colours = colours.reshape(9, local_rows // 2, half_cols)
     stencil = by_offset(colours, row_start // 2, col_start // 2)
-    moved = lax.all_to_all(stencil, "gx", split_axis=1, concat_axis=2, tiled=True)
+    moved = settle_the_joints(stencil, "gx", 1, frame_in=2)
     return moved[:, None]
 
 

time: 212 us -> 192 us (0.906)
  the two profiles are of different devices: /device:TPU:4 before, /device:TPU:13 now
where the time goes in v1:
time: 192 us; the launch traced here: 191 us
  local copies, waits for them, and re-layouts  74.6 us (39%)
  other arithmetic  46.7 us (24%)
  waiting for transfers between devices  30.7 us (16%)
  loops' own time  19 us (10%)
  starting transfers between devices  14.9 us (8%)
  matrix products  4.33 us (2%)
    ppermute x3, waiting for transfers between devices, settle_the_joints(): ppermute(local_now, ax_name, [(s, (s + d) % y) for s in range(y)])  26.2 us
    while x90, local copies, waits for them, and re-layouts  21.7 us
    another operation x1, loops' own time, shards(): lax.map(partial(probe_rows, prepared, local_rows), jnp.arange(9, dtype=jn...  19 us
    mul x9, other arithmetic, probe_rows(): vertical * fine_field  12.9 us
    broadcast_in_dim x9, local copies, waits for them, and re-layouts, shards(): lax.map(partial(probe_rows, prepared, local_rows), jnp.arange(9, dtype=jn...  11.4 us
    reshape x9, local copies, waits for them, and re-layouts, probe_rows(): kept = cols_done[2:2 + local_rows].reshape(local_rows // 2, 2, width)  10.5 us
    ppermute x2, starting transfers between devices, with_halo(): lax.ppermute(tail, axis, [(i, (i + 1) % count) for i in range(ends)])  8.31 us
    sub x9, other arithmetic, probe_rows(): centre * fine_field - east_face * jnp.roll(fine_field, -1, 1)  6.98 us
  transfers between devices with their start and end apart: 7, of which 5 were waited for; matrix products, arithmetic and copies ran while one was open for 1% of the time, Pallas kernels for 0%

profile of v1, /device:TPU:13, one launch (start us, length us, event | category | flops | bytes accessed | tf_op | source)
XLA Modules:
  0.0 190.8 jit_solution(17581879478218706947)
XLA Ops:
  0.0 1.0 fusion.80
  1.0 3.2 %collective-permute-start = (bf16[2,128,2]{2,1,0:T(8,128)(2,1)S(1)}, bf16[2,128,2]{2,1,0:T(8,128)(2,1)S(1)}, u32[]{:S(2)}, u32[]{:S(2)}) collective-permute-start(bf16[2,128,2]{2,1,0:T(8,128)(2,1)S(1)} %get-tuple-element.446), channel_id=1, source_target_pairs={{0,8},{8,16},{16,24},{1,9},{9,17},{17,25},{2,10},{10,18},{18,26},{... | collective-permute-start | bytes 3080 | tf_op jit(solution)/shard_map/ppermute | solution.py:38
  4.2 2.1 %collective-permute-start.1 = (bf16[2,128,2]{2,1,0:T(8,128)(2,1)S(1)}, bf16[2,128,2]{2,1,0:T(8,128)(2,1)S(1)}, u32[]{:S(2)}, u32[]{:S(2)}) collective-permute-start(bf16[2,128,2]{2,1,0:T(8,128)(2,1)S(1)} %get-tuple-element.445), channel_id=1, source_target_pairs={{8,0},{16,8},{24,16},{9,1},{17,9},{25,17},{10,2},{18,10},{26,18},{... | collective-permute-start | bytes 3080 | tf_op jit(solution)/shard_map/ppermute | solution.py:40
  7.6 1.6 collective-permute-done.1
  9.8 5.1 %collective-permute-start.2 = (bf16[2,2,1028]{2,1,0:T(2,128)(2,1)S(1)}, bf16[2,2,1028]{2,1,0:T(2,128)(2,1)S(1)}, u32[]{:S(2)}, u32[]{:S(2)}) collective-permute-start(bf16[2,2,1028]{2,1,0:T(2,128)(2,1)S(1)} %get-tuple-element.443), channel_id=1, source_target_pairs={{0,1},{1,2},{2,3},{3,4},{4,5},{5,6},{6,7},{8,9},{9,10},{10,11},{11... | collective-permute-start | bytes 24680 | tf_op jit(solution)/shard_map/ppermute | solution.py:38
  14.9 1.9 %collective-permute-start.3 = (bf16[2,2,1028]{2,1,0:T(2,128)(2,1)S(1)}, bf16[2,2,1028]{2,1,0:T(2,128)(2,1)S(1)}, u32[]{:S(2)}, u32[]{:S(2)}) collective-permute-start(bf16[2,2,1028]{2,1,0:T(2,128)(2,1)S(1)} %get-tuple-element.444), channel_id=1, source_target_pairs={{1,0},{2,1},{3,2},{4,3},{5,4},{6,5},{7,6},{9,8},{10,9},{11,10},{12... | collective-permute-start | bytes 24680 | tf_op jit(solution)/shard_map/ppermute | solution.py:40
  17.0 3.0 %collective-permute-done.3 = bf16[2,2,1028]{2,1,0:T(2,128)(2,1)S(1)} collective-permute-done((bf16[2,2,1028]{2,1,0:T(2,128)(2,1)S(1)}, bf16[2,2,1028]{2,1,0:T(2,128)(2,1)S(1)}, u32[]{:S(2)}, u32[]{:S(2)}) %collective-permute-start.3) | collective-permute-done | bytes 8256 | tf_op jit(solution)/shard_map/ppermute | solution.py:40
  21.0 0.9 fusion.39
  22.0 4.1 %add_add_fusion = (f32[2,136,1152]{2,1,0:T(8,128)}, f32[2,136,1152]{2,1,0:T(8,128)S(1)}, f32[2,136,1152]{2,1,0:T(8,128)S(1)}, f32[2,136,1152]{2,1,0:T(8,128)S(1)}, f32[2,136,1152]{2,1,0:T(8,128)S(1)}) fusion(f32[136,1152]{1,0:T(8,128)S(1)} %divide_bitcast_fusion, pred[136,1152]{1,0:T(8,128)(4,1)S(1)} %broadcast_and_fusion, ...), kind=kLoop, calls=%fused_computation.67 | loop fusion | flops 13160448 | bytes 13233216 | tf_op jit(solution)/shard_map/add | solution.py:84
  26.3 0.9 copy-done
  28.5 123.6 %while.14 = (s32[]{:T(128)}, f32[9,64,1152]{2,1,0:T(8,128)}, s32[9]{0:T(128)S(1)}, f32[136,1152]{1,0:T(8,128)S(1)}, f32[136,1152]{1,0:T(8,128)S(1)}, /*index=5*/...) while((s32[]{:T(128)}, f32[9,64,1152]{2,1,0:T(8,128)}, ...), condition=%wide.region_1.2_spmd.clone.clone, body=%wide.region_0.1_spmd.clone.clone.sunk | while | flops 10339566 | bytes 78140304 | solution.py:217
  32.3 1.4 fusion.106
  34.7 0.8 copy-done.8
  37.1 0.8 subtract_subtract_fusion.2
  39.0 1.2 reshape.783
  40.2 1.3 slice_bitcast_fusion.2
  46.0 1.4 fusion.106
  48.4 0.8 copy-done.8
  50.8 0.8 subtract_subtract_fusion.2
  52.8 1.2 reshape.783
  53.9 1.3 slice_bitcast_fusion.2
  59.8 1.4 fusion.106
  62.1 0.8 copy-done.8
  64.5 0.8 subtract_subtract_fusion.2
  66.5 1.2 reshape.783
  67.7 1.3 slice_bitcast_fusion.2
  73.5 1.4 fusion.106
  75.9 0.8 copy-done.8
  78.3 0.8 subtract_subtract_fusion.2
  80.3 1.2 reshape.783
  81.4 1.3 slice_bitcast_fusion.2
  87.3 1.4 fusion.106
  89.6 0.8 copy-done.8
  92.0 0.8 subtract_subtract_fusion.2
  94.0 1.2 reshape.783
  95.2 1.3 slice_bitcast_fusion.2
  101.0 1.4 fusion.106
  103.4 0.8 copy-done.8
  105.8 0.8 subtract_subtract_fusion.2
  107.7 1.2 reshape.783
  108.9 1.3 slice_bitcast_fusion.2
  114.7 1.4 fusion.106
  117.1 0.8 copy-done.8
  119.5 0.8 subtract_subtract_fusion.2
  121.4 1.2 reshape.783
  122.6 1.3 slice_bitcast_fusion.2
  128.4 1.4 fusion.106
  130.8 0.8 copy-done.8
  133.2 0.8 subtract_subtract_fusion.2
  135.2 1.2 reshape.783
  136.3 1.3 slice_bitcast_fusion.2
  142.2 1.4 fusion.106
  144.5 0.8 copy-done.8
  146.9 0.8 subtract_subtract_fusion.2
  148.9 1.2 reshape.783
  150.1 1.3 slice_bitcast_fusion.2
  152.1 4.3 %fusion.23 = f32[576,512]{1,0:T(8,128)S(1)} fusion(f32[576,1152]{1,0:T(8,128)} %bitcast.103, s32[512]{0:T(512)S(1)} %multiply_add_fusion), kind=kOutput, calls=%fused_computation.56 | convolution fusion | flops 4077453312 | bytes 3835904 | tf_op jit(solution)/shard_map/dot_general | solution.py:225
  158.7 1.3 collective-permute-start.4
  160.0 1.0 collective-permute-start.5
  161.3 6.2 %collective-permute-done.4 = f32[9,16,512]{2,1,0:T(8,128)S(1)} collective-permute-done((f32[9,16,512]{2,1,0:T(8,128)S(1)}, f32[9,16,512]{2,1,0:T(8,128)S(1)}, u32[]{:S(2)}, u32[]{:S(2)}) %collective-permute-start.4) | collective-permute-done | bytes 294944 | tf_op jit(solution)/shard_map/ppermute | solution.py:198
  167.4 18.0 %collective-permute-done.5 = f32[9,16,512]{2,1,0:T(8,128)S(1)} collective-permute-done((f32[9,16,512]{2,1,0:T(8,128)S(1)}, f32[9,16,512]{2,1,0:T(8,128)S(1)}, u32[]{:S(2)}, u32[]{:S(2)}) %collective-permute-start.5) | collective-permute-done | bytes 294944 | tf_op jit(solution)/shard_map/ppermute | solution.py:198
  185.5 2.0 %collective-permute-done.6 = f32[9,16,512]{2,1,0:T(8,128)S(1)} collective-permute-done((f32[9,16,512]{2,1,0:T(8,128)S(1)}, f32[9,16,512]{2,1,0:T(8,128)S(1)}, u32[]{:S(2)}, u32[]{:S(2)}) %collective-permute-start.6) | collective-permute-done | bytes 294944 | tf_op jit(solution)/shard_map/ppermute | solution.py:198
  188.2 0.8 copy.3
  189.0 1.8 broadcast_in_dim_reshape.3
  (411 shorter events, 63.1 us)
Async XLA Ops:
  1.0 6.7 %collective-permute-start = (bf16[2,128,2]{2,1,0:T(8,128)(2,1)S(1)}, bf16[2,128,2]{2,1,0:T(8,128)(2,1)S(1)}, u32[]{:S(2)}, u32[]{:S(2)}) collective-permute-start(bf16[2,128,2]{2,1,0:T(8,128)(2,1)S(1)} %get-tuple-element.446), channel_id=1, source_target_pairs={{0,8},{8,16},{16,24},{1,9},{9,17},{17,25},{2,10},{10,18},{18,26},{... | collective-permute-start | bytes 3080 | tf_op jit(solution)/shard_map/ppermute | solution.py:38
  4.2 5.0 %collective-permute-start.1 = (bf16[2,128,2]{2,1,0:T(8,128)(2,1)S(1)}, bf16[2,128,2]{2,1,0:T(8,128)(2,1)S(1)}, u32[]{:S(2)}, u32[]{:S(2)}) collective-permute-start(bf16[2,128,2]{2,1,0:T(8,128)(2,1)S(1)} %get-tuple-element.445), channel_id=1, source_target_pairs={{8,0},{16,8},{24,16},{9,1},{17,9},{25,17},{10,2},{18,10},{26,18},{... | collective-permute-start | bytes 3080 | tf_op jit(solution)/shard_map/ppermute | solution.py:40
  6.5 2.7 %copy-start.9 = (bf16[2,128,1024]{2,1,0:T(8,128)(2,1)S(1)}, bf16[2,128,1024]{2,1,0:T(8,128)(2,1)}, u32[]{:S(2)}) copy-start(bf16[2,128,1024]{2,1,0:T(8,128)(2,1)} %param.3) | copy-start | bytes 1572868
  9.8 7.1 %collective-permute-start.2 = (bf16[2,2,1028]{2,1,0:T(2,128)(2,1)S(1)}, bf16[2,2,1028]{2,1,0:T(2,128)(2,1)S(1)}, u32[]{:S(2)}, u32[]{:S(2)}) collective-permute-start(bf16[2,2,1028]{2,1,0:T(2,128)(2,1)S(1)} %get-tuple-element.443), channel_id=1, source_target_pairs={{0,1},{1,2},{2,3},{3,4},{4,5},{5,6},{6,7},{8,9},{9,10},{10,11},{11... | collective-permute-start | bytes 24680 | tf_op jit(solution)/shard_map/ppermute | solution.py:38
  14.9 5.0 %collective-permute-start.3 = (bf16[2,2,1028]{2,1,0:T(2,128)(2,1)S(1)}, bf16[2,2,1028]{2,1,0:T(2,128)(2,1)S(1)}, u32[]{:S(2)}, u32[]{:S(2)}) collective-permute-start(bf16[2,2,1028]{2,1,0:T(2,128)(2,1)S(1)} %get-tuple-element.444), channel_id=1, source_target_pairs={{1,0},{2,1},{3,2},{4,3},{5,4},{6,5},{7,6},{9,8},{10,9},{11,10},{12... | collective-permute-start | bytes 24680 | tf_op jit(solution)/shard_map/ppermute | solution.py:40
  26.1 1.0 copy-start
  26.1 1.5 copy-start.2
  26.1 2.0 %copy-start.4 = (f32[2,136,1152]{2,1,0:T(8,128)}, f32[2,136,1152]{2,1,0:T(8,128)S(1)}, u32[]{:S(2)}) copy-start(f32[2,136,1152]{2,1,0:T(8,128)S(1)} %get-tuple-element.650) | copy-start | bytes 3760132
  26.1 2.4 %copy-start.6 = (f32[2,136,1152]{2,1,0:T(8,128)}, f32[2,136,1152]{2,1,0:T(8,128)S(1)}, u32[]{:S(2)}) copy-start(f32[2,136,1152]{2,1,0:T(8,128)S(1)} %get-tuple-element.651) | copy-start | bytes 3760132
  34.2 1.3 copy-start.8
  34.4 1.5 copy-start.5
  34.4 1.9 copy-start.7
  34.5 2.2 %copy-start.1 = (f32[2,136,1152]{2,1,0:T(8,128)S(1)}, f32[2,136,1152]{2,1,0:T(8,128)}, u32[]{:S(2)}) copy-start(f32[2,136,1152]{2,1,0:T(8,128)} %get-tuple-element.702) | copy-start | bytes 3760132 | tf_op jit(solution)/shard_map/while
  34.5 2.5 %copy-start.3 = (f32[2,136,1152]{2,1,0:T(8,128)S(1)}, f32[2,136,1152]{2,1,0:T(8,128)}, u32[]{:S(2)}) copy-start(f32[2,136,1152]{2,1,0:T(8,128)} %get-tuple-element.703) | copy-start | bytes 3760132 | tf_op jit(solution)/shard_map/while
  47.9 1.3 copy-start.8
  48.1 1.5 copy-start.5
  48.2 1.9 copy-start.7
  48.3 2.2 %copy-start.1 = (f32[2,136,1152]{2,1,0:T(8,128)S(1)}, f32[2,136,1152]{2,1,0:T(8,128)}, u32[]{:S(2)}) copy-start(f32[2,136,1152]{2,1,0:T(8,128)} %get-tuple-element.702) | copy-start | bytes 3760132 | tf_op jit(solution)/shard_map/while
  48.3 2.5 %copy-start.3 = (f32[2,136,1152]{2,1,0:T(8,128)S(1)}, f32[2,136,1152]{2,1,0:T(8,128)}, u32[]{:S(2)}) copy-start(f32[2,136,1152]{2,1,0:T(8,128)} %get-tuple-element.703) | copy-start | bytes 3760132 | tf_op jit(solution)/shard_map/while
  61.7 1.3 copy-start.8
  61.9 1.5 copy-start.5
  61.9 1.9 copy-start.7
  62.0 2.2 %copy-start.1 = (f32[2,136,1152]{2,1,0:T(8,128)S(1)}, f32[2,136,1152]{2,1,0:T(8,128)}, u32[]{:S(2)}) copy-start(f32[2,136,1152]{2,1,0:T(8,128)} %get-tuple-element.702) | copy-start | bytes 3760132 | tf_op jit(solution)/shard_map/while
  62.0 2.5 %copy-start.3 = (f32[2,136,1152]{2,1,0:T(8,128)S(1)}, f32[2,136,1152]{2,1,0:T(8,128)}, u32[]{:S(2)}) copy-start(f32[2,136,1152]{2,1,0:T(8,128)} %get-tuple-element.703) | copy-start | bytes 3760132 | tf_op jit(solution)/shard_map/while
  75.4 1.3 copy-start.8
  75.6 1.5 copy-start.5
  75.6 1.9 copy-start.7
  75.8 2.2 %copy-start.1 = (f32[2,136,1152]{2,1,0:T(8,128)S(1)}, f32[2,136,1152]{2,1,0:T(8,128)}, u32[]{:S(2)}) copy-start(f32[2,136,1152]{2,1,0:T(8,128)} %get-tuple-element.702) | copy-start | bytes 3760132 | tf_op jit(solution)/shard_map/while
  75.8 2.5 %copy-start.3 = (f32[2,136,1152]{2,1,0:T(8,128)S(1)}, f32[2,136,1152]{2,1,0:T(8,128)}, u32[]{:S(2)}) copy-start(f32[2,136,1152]{2,1,0:T(8,128)} %get-tuple-element.703) | copy-start | bytes 3760132 | tf_op jit(solution)/shard_map/while
  89.1 1.3 copy-start.8
  89.4 1.5 copy-start.5
  89.4 1.9 copy-start.7
  89.5 2.2 %copy-start.1 = (f32[2,136,1152]{2,1,0:T(8,128)S(1)}, f32[2,136,1152]{2,1,0:T(8,128)}, u32[]{:S(2)}) copy-start(f32[2,136,1152]{2,1,0:T(8,128)} %get-tuple-element.702) | copy-start | bytes 3760132 | tf_op jit(solution)/shard_map/while
  89.5 2.5 %copy-start.3 = (f32[2,136,1152]{2,1,0:T(8,128)S(1)}, f32[2,136,1152]{2,1,0:T(8,128)}, u32[]{:S(2)}) copy-start(f32[2,136,1152]{2,1,0:T(8,128)} %get-tuple-element.703) | copy-start | bytes 3760132 | tf_op jit(solution)/shard_map/while
  102.9 1.3 copy-start.8
  103.1 1.5 copy-start.5
  103.1 1.9 copy-start.7
  103.2 2.2 %copy-start.1 = (f32[2,136,1152]{2,1,0:T(8,128)S(1)}, f32[2,136,1152]{2,1,0:T(8,128)}, u32[]{:S(2)}) copy-start(f32[2,136,1152]{2,1,0:T(8,128)} %get-tuple-element.702) | copy-start | bytes 3760132 | tf_op jit(solution)/shard_map/while
  103.2 2.5 %copy-start.3 = (f32[2,136,1152]{2,1,0:T(8,128)S(1)}, f32[2,136,1152]{2,1,0:T(8,128)}, u32[]{:S(2)}) copy-start(f32[2,136,1152]{2,1,0:T(8,128)} %get-tuple-element.703) | copy-start | bytes 3760132 | tf_op jit(solution)/shard_map/while
  116.6 1.3 copy-start.8
  116.8 1.5 copy-start.5
  116.8 1.9 copy-start.7
  116.9 2.2 %copy-start.1 = (f32[2,136,1152]{2,1,0:T(8,128)S(1)}, f32[2,136,1152]{2,1,0:T(8,128)}, u32[]{:S(2)}) copy-start(f32[2,136,1152]{2,1,0:T(8,128)} %get-tuple-element.702) | copy-start | bytes 3760132 | tf_op jit(solution)/shard_map/while
  117.0 2.5 %copy-start.3 = (f32[2,136,1152]{2,1,0:T(8,128)S(1)}, f32[2,136,1152]{2,1,0:T(8,128)}, u32[]{:S(2)}) copy-start(f32[2,136,1152]{2,1,0:T(8,128)} %get-tuple-element.703) | copy-start | bytes 3760132 | tf_op jit(solution)/shard_map/while
  130.3 1.3 copy-start.8
  130.5 1.5 copy-start.5
  130.5 1.9 copy-start.7
  130.7 2.2 %copy-start.1 = (f32[2,136,1152]{2,1,0:T(8,128)S(1)}, f32[2,136,1152]{2,1,0:T(8,128)}, u32[]{:S(2)}) copy-start(f32[2,136,1152]{2,1,0:T(8,128)} %get-tuple-element.702) | copy-start | bytes 3760132 | tf_op jit(solution)/shard_map/while
  130.7 2.5 %copy-start.3 = (f32[2,136,1152]{2,1,0:T(8,128)S(1)}, f32[2,136,1152]{2,1,0:T(8,128)}, u32[]{:S(2)}) copy-start(f32[2,136,1152]{2,1,0:T(8,128)} %get-tuple-element.703) | copy-start | bytes 3760132 | tf_op jit(solution)/shard_map/while
  144.0 1.3 copy-start.8
  144.3 1.5 copy-start.5
  144.3 1.9 copy-start.7
  144.4 2.2 %copy-start.1 = (f32[2,136,1152]{2,1,0:T(8,128)S(1)}, f32[2,136,1152]{2,1,0:T(8,128)}, u32[]{:S(2)}) copy-start(f32[2,136,1152]{2,1,0:T(8,128)} %get-tuple-element.702) | copy-start | bytes 3760132 | tf_op jit(solution)/shard_map/while
  144.4 2.5 %copy-start.3 = (f32[2,136,1152]{2,1,0:T(8,128)S(1)}, f32[2,136,1152]{2,1,0:T(8,128)}, u32[]{:S(2)}) copy-start(f32[2,136,1152]{2,1,0:T(8,128)} %get-tuple-element.703) | copy-start | bytes 3760132 | tf_op jit(solution)/shard_map/while
  158.7 8.8 %collective-permute-start.4 = (f32[9,16,512]{2,1,0:T(8,128)S(1)}, f32[9,16,512]{2,1,0:T(8,128)S(1)}, u32[]{:S(2)}, u32[]{:S(2)}) collective-permute-start(f32[9,16,512]{2,1,0:T(8,128)S(1)} %get-tuple-element.442), channel_id=1, source_target_pairs={{0,8},{8,16},{16,24},{24,0},{1,9},{9,17},{17,25},{25,1},{2,10},{10... | collective-permute-start | bytes 884744 | tf_op jit(solution)/shard_map/ppermute | solution.py:198
  160.0 25.5 %collective-permute-start.5 = (f32[9,16,512]{2,1,0:T(8,128)S(1)}, f32[9,16,512]{2,1,0:T(8,128)S(1)}, u32[]{:S(2)}, u32[]{:S(2)}) collective-permute-start(f32[9,16,512]{2,1,0:T(8,128)S(1)} %get-tuple-element.441), channel_id=1, source_target_pairs={{0,16},{8,24},{16,0},{24,8},{1,17},{9,25},{17,1},{25,9},{2,18},{10... | collective-permute-start | bytes 884744 | tf_op jit(solution)/shard_map/ppermute | solution.py:198
  161.0 26.5 %collective-permute-start.6 = (f32[9,16,512]{2,1,0:T(8,128)S(1)}, f32[9,16,512]{2,1,0:T(8,128)S(1)}, u32[]{:S(2)}, u32[]{:S(2)}) collective-permute-start(f32[9,16,512]{2,1,0:T(8,128)S(1)} %get-tuple-element.440), channel_id=1, source_target_pairs={{0,24},{8,0},{16,8},{24,16},{1,25},{9,1},{17,9},{25,17},{2,26},{10... | collective-permute-start | bytes 884744 | tf_op jit(solution)/shard_map/ppermute | solution.py:198
